TPU v7x, 32 devices: a whole 2x2x4 slice. The times are simulated.
32 devices in a mesh: heads: 2 (over core), blk: 16 (over z, y, x).
Axes of the slice: x: 2, y: 2, z: 4, core: 2. Of those that a mesh axis runs over, the one named last changes fastest.
Arguments:
- queries: bfloat16 [3072, 4096], P('blk', 'heads'), may hold values from -8 to 8
- keys: bfloat16 [3072, 4096], P('blk', 'heads'), may hold values from -6 to 6
- values: bfloat16 [3072, 4096], P('blk', 'heads'), may hold values from -24 to 24
- prefix_keys: bfloat16 [1024, 4096], P('blk', 'heads'), may hold values from -8 to 8
- prefix_values: bfloat16 [1024, 4096], P('blk', 'heads'), may hold values from -24 to 24
- lengths: int32 [24], replicated, may hold values from 1 to 224, 3072 in all
- groups: int32 [24], replicated, may hold values from 0 to 3, as said below
- out_weight: bfloat16 [4096, 4096], P('heads'), may hold values from -0.09375 to 0.09375
Outputs:
- attn_branch: bfloat16 [3072, 4096], P('blk', 'heads')
Inputs may be any that keep to these rules, and one draw needn't show every extreme that they name: Each of the 4 groups holds 6 requests. The lengths sum to 3072; the longest is 224.
All inputs are finite; a program needn't handle non-finite values.
Results may differ from a plain program's by a relative error of at most 0.019.
Values may be sent and summed in bfloat16 or wider, within the bound.
A program may use at most 128 MiB of HBM per device.

v0:
```python
import math
import jax
import jax.numpy as jnp
from jax import lax
from jax.sharding import PartitionSpec as P

HD = 128
ROT = 32
GROUPS = 4
MOST = 224


def shifted(block, axis, distance):
    devices = range(lax.axis_size(axis))
    route = [(i - distance, i) for i in devices if i - distance in devices]
    return lax.ppermute(block, axis, route)


def token_tables(lengths, groups, tok_index, prefix_len):
    ends = jnp.cumsum(lengths)
    starts = ends - lengths
    inside = (starts[None, :] <= tok_index[:, None]) & (tok_index[:, None] < ends[None, :])
    start_tok = jnp.sum(jnp.where(inside, starts[None, :] + 1, 0), axis=1) - 1
    group_tok = jnp.sum(jnp.where(inside, groups[None, :], 0), axis=1)
    position = prefix_len + tok_index - start_tok
    return (start_tok, group_tok, position)


def rotary(field, position):
    half = ROT // 2
    inverse = 10000.0 ** (-(jnp.arange(half, dtype=jnp.float32) * 2.0 / ROT))
    angle = position.astype(jnp.float32)[:, None] * inverse[None, :]
    angle = jnp.concatenate([angle, angle], axis=1)
    cosine = jnp.cos(angle)[:, None, :]
    sine = jnp.sin(angle)[:, None, :]
    front = field[..., :ROT]
    turned = jnp.concatenate([-front[..., half:], front[..., :half]], axis=-1)
    rotated = front * cosine + turned * sine
    return jnp.concatenate([rotated, field[..., ROT:]], axis=-1)


def online_update(state, q_rot, key_rows, value_rows, mask, scale):
    top_old, total_old, accum_old = state
    score = jnp.einsum("qhd,khd->hqk", q_rot, key_rows, preferred_element_type=jnp.float32) * scale
    score = jnp.where(mask[None], score, -1e30)
    top_new = jnp.maximum(top_old, jnp.max(score, axis=-1))
    expo = jnp.exp(score - top_new[..., None])
    factor = jnp.exp(top_old - top_new)
    total_new = total_old * factor + jnp.sum(expo, axis=-1)
    weights = expo.astype(jnp.bfloat16)
    accum_new = accum_old * factor[..., None] + jnp.einsum(
        "hqk,khd->hqd", weights, value_rows, preferred_element_type=jnp.float32
    )
    return (top_new, total_new, accum_new)


def body(queries, keys, values, prefix_keys, prefix_values, lengths, groups, out_weight):
    tok = queries.shape[0]
    width = queries.shape[1]
    heads_dev = width // HD
    scale = 1.0 / math.sqrt(HD)
    n_blk = lax.axis_size("blk")
    prefix_len = prefix_keys.shape[0] * n_blk // GROUPS
    first = lax.axis_index("blk") * tok
    tok_index = first + jnp.arange(tok, dtype=jnp.int32)
    start_tok, group_tok, position = token_tables(lengths, groups, tok_index, prefix_len)
    q_rot = rotary(queries.reshape(tok, heads_dev, HD).astype(jnp.float32), position).astype(
        jnp.bfloat16
    )
    k_rot = rotary(keys.reshape(tok, heads_dev, HD).astype(jnp.float32), position).astype(
        jnp.bfloat16
    )
    v_own = values.reshape(tok, heads_dev, HD)
    span = (MOST - 2) // tok + 1
    key_list = [k_rot]
    value_list = [v_own]
    index_list = [tok_index]
    for distance in range(1, span + 1):
        moved_k, moved_v = shifted((k_rot, v_own), "blk", distance)
        key_list = [moved_k] + key_list
        value_list = [moved_v] + value_list
        index_list = [tok_index - distance * tok] + index_list
    near_k = jnp.concatenate(key_list, axis=0)
    near_v = jnp.concatenate(value_list, axis=0)
    near_index = jnp.concatenate(index_list, axis=0)
    near_start = token_tables(lengths, groups, near_index, prefix_len)[0]
    near_mask = (near_start[None, :] == start_tok[:, None]) & (
        near_index[None, :] <= tok_index[:, None]
    )
    state = (
        jnp.full((heads_dev, tok), -1e30, jnp.float32),
        jnp.zeros((heads_dev, tok), jnp.float32),
        jnp.zeros((heads_dev, tok, HD), jnp.float32),
    )
    state = online_update(state, q_rot, near_k, near_v, near_mask, scale)
    piece_k = lax.all_gather(prefix_keys, "blk", axis=0, tiled=True)
    piece_v = lax.all_gather(prefix_values, "blk", axis=0, tiled=True)
    count = piece_k.shape[0]
    row_group = jnp.arange(count, dtype=jnp.int32) // prefix_len
    mask = row_group[None, :] == group_tok[:, None]
    top_final, total_final, accum_final = online_update(
        state,
        q_rot,
        piece_k.reshape(count, heads_dev, HD),
        piece_v.reshape(count, heads_dev, HD),
        mask,
        scale,
    )
    attn = accum_final / total_final[..., None]
    attn = jnp.transpose(attn, (1, 0, 2)).reshape(tok, width).astype(jnp.bfloat16)
    partial_out = jnp.dot(attn, out_weight, preferred_element_type=jnp.float32)
    projected = lax.psum_scatter(
        partial_out.astype(jnp.bfloat16), "heads", scatter_dimension=1, tiled=True
    )
    return projected


def solution(mesh):
    placed = (
        P("blk", "heads"),
        P("blk", "heads"),
        P("blk", "heads"),
        P("blk", "heads"),
        P("blk", "heads"),
        P(),
        P(),
        P("heads", None),
    )
    return jax.shard_map(
        body, mesh=mesh, in_specs=placed, out_specs=P("blk", "heads"), check_vma=False
    )
```

profile of v0, /device:TPU:0, one launch (start us, length us, event | category | flops | bytes accessed | tf_op | source)
XLA Modules:
  0.0 262.7 jit_solution(15285865329272532625)
XLA Ops:
  6.5 0.7 all-gather.3.cloned.1.call-update
  7.3 0.0 all-gather.5.cloned.1.call-start
  7.3 0.7 all-gather.5.cloned.1.call-update
  8.0 0.0 reduce-scatter.2.cloned.1.call-start
  8.1 0.7 copy.44
  8.8 0.1 reduce
  9.0 0.7 broadcast_add_fusion.2
  9.6 0.7 select_reduce_fusion.1
  10.4 0.1 broadcast_multiply_fusion
  10.5 0.1 fusion.51
  10.6 0.1 copy.46
  10.7 0.1 copy.47
  10.8 0.3 fusion.70
  11.1 0.3 slice.45
  11.4 0.3 fusion.69
  11.6 1.2 slice_negate_fusion
  12.8 0.0 copy-start.3
  12.8 1.0 fusion.32
  13.8 0.4 pad_maximum_fusion.1
  14.3 4.9 %collective-permute-start = (bf16[192,16,128]{2,0,1:T(8,128)(2,1)S(1)}, bf16[192,16,128]{2,0,1:T(8,128)(2,1)S(1)}, u32[]{:S(2)}, u32[]{:S(2)}) collective-permute-start(bf16[192,16,128]{2,0,1:T(8,128)(2,1)S(1)} %pad_maximum_fusion.1), channel_id=1, source_target_pairs={{0,2},{1,3},{2,4},{3,5},{4,6},{5,7},{6,8},{7,9},{8,10},{9,11},{10,... | collective-permute-start | bytes 2359304 | tf_op jit(solution)/shard_map/ppermute | solution.py:16
  19.2 3.4 %collective-permute-start.1 = (bf16[192,16,128]{2,0,1:T(8,128)(2,1)S(1)}, bf16[192,16,128]{2,0,1:T(8,128)(2,1)S(1)}, u32[]{:S(2)}, u32[]{:S(2)}) collective-permute-start(bf16[192,16,128]{2,0,1:T(8,128)(2,1)S(1)} %pad_maximum_fusion.1), channel_id=1, source_target_pairs={{0,1},{1,2},{2,3},{3,4},{4,5},{5,6},{6,7},{7,8},{8,9},{9,10},{10,1... | collective-permute-start | bytes 2359304 | tf_op jit(solution)/shard_map/ppermute | solution.py:16
  22.7 0.2 copy_bitcast_fusion
  22.9 4.3 %collective-permute-start.2 = (bf16[192,16,128]{2,0,1:T(8,128)(2,1)S(1)}, bf16[192,16,128]{2,0,1:T(8,128)(2,1)}, u32[]{:S(2)}, u32[]{:S(2)}) collective-permute-start(bf16[192,16,128]{2,0,1:T(8,128)(2,1)S(1)} %copy_bitcast_fusion), channel_id=1, source_target_pairs={{0,2},{1,3},{2,4},{3,5},{4,6},{5,7},{6,8},{7,9},{8,10},{9,11},{10,... | collective-permute-start | bytes 2359304 | tf_op jit(solution)/shard_map/ppermute | solution.py:16
  27.1 4.3 %collective-permute-start.3 = (bf16[192,16,128]{2,0,1:T(8,128)(2,1)S(1)}, bf16[192,16,128]{2,0,1:T(8,128)(2,1)}, u32[]{:S(2)}, u32[]{:S(2)}) collective-permute-start(bf16[192,16,128]{2,0,1:T(8,128)(2,1)S(1)} %copy_bitcast_fusion), channel_id=1, source_target_pairs={{0,1},{1,2},{2,3},{3,4},{4,5},{5,6},{6,7},{7,8},{8,9},{9,10},{10,1... | collective-permute-start | bytes 2359304 | tf_op jit(solution)/shard_map/ppermute | solution.py:16
  31.4 0.3 slice.41
  31.7 0.1 pad_add_fusion
  31.8 0.1 select_reduce_fusion
  31.9 0.2 compare_and_fusion
  32.1 0.2 broadcast_compare_fusion
  32.3 40.4 %collective-permute-done = bf16[192,16,128]{2,0,1:T(8,128)(2,1)S(1)} collective-permute-done((bf16[192,16,128]{2,0,1:T(8,128)(2,1)S(1)}, bf16[192,16,128]{2,0,1:T(8,128)(2,1)S(1)}, u32[]{:S(2)}, u32[]{:S(2)}) %collective-permute-start) | collective-permute-done | bytes 786464 | tf_op jit(solution)/shard_map/ppermute | solution.py:16
  72.6 0.0 collective-permute-done.1
  72.6 4.8 %fusion.3 = (f32[16,192]{1,0:T(8,128)S(1)}, f32[16,192,576]{2,1,0:T(8,128)}) fusion(pred[192,576]{1,0:T(8,128)(4,1)S(1)} %compare_and_fusion, bf16[192,16,96]{2,0,1:T(8,128)(2,1)S(1)} %slice.45, bf16[192,16,32]{2,0,1:T(8,128)(2,1)S(1)} %get-tuple-element.19, bf16[192,16,128]{2,0,1:T(8,128)(2,1)S(1)} %collective-permute-done.1, ...), kind=kOutput, calls=%fused_computation.7 | convolution fusion | flops 469300224 | bytes 10346496 | tf_op jit(solution)/shard_map/qhd,khd->hqk/dot_general | solution.py:44
  77.5 64.7 %all-gather.3.cloned.1.call-done = bf16[1024,2048]{1,0:T(8,128)(2,1)} async-done(((bf16[64,2048]{1,0:T(8,128)(2,1)}), bf16[1024,2048]{1,0:T(8,128)(2,1)}) %all-gather.3.cloned.1.call-update) | async-done | bytes 4194320 | tf_op jit(solution)/shard_map/all_gather | solution.py:96
  142.1 6.4 %copy.54 = bf16[1024,2048]{0,1:T(8,128)(2,1)} copy(bf16[1024,2048]{1,0:T(8,128)(2,1)} %all-gather.3.cloned.1.call-done) | data formatting | bytes 8388608 | tf_op jit(solution)/shard_map/all_gather | solution.py:96
  148.6 5.2 %fusion = (f32[16,192]{1,0:T(8,128)S(1)}, f32[16,192,1024]{2,1,0:T(8,128)S(1)}) fusion(pred[192,1024]{1,0:T(8,128)(4,1)S(1)} %broadcast_compare_fusion, bf16[1024,16,128]{0,2,1:T(8,128)(2,1)} %bitcast.67, bf16[192,16,96]{2,0,1:T(8,128)(2,1)S(1)} %slice.41, bf16[192,16,32]{2,0,1:T(8,128)(2,1)S(1)} %get-tuple-element.20), kind=kOutput, calls=%fused_computation.2 | convolution fusion | flops 816313344 | bytes 17772544 | tf_op jit(solution)/shard_map/qhd,khd->hqk/dot_general | solution.py:44
  153.8 0.0 slice-done
  153.8 2.3 fusion.10
  156.2 3.6 %fusion.1 = f32[16,192]{1,0:T(8,128)S(1)} fusion(f32[16,192,1024]{2,1,0:T(8,128)S(1)} %get-tuple-element.31, f32[16,192]{1,0:T(8,128)S(1)} %get-tuple-element.23, pred[192,1024]{1,0:T(8,128)(4,1)S(1)} %broadcast_compare_fusion), kind=kLoop, calls=%fused_computation.3 | loop fusion | flops 12579840 | bytes 12804096 | tf_op jit(solution)/shard_map/reduce_sum | solution.py:49
  159.8 58.2 %all-gather.5.cloned.1.call-done = bf16[1024,2048]{1,0:T(8,128)(2,1)} async-done(((bf16[64,2048]{1,0:T(8,128)(2,1)}), bf16[1024,2048]{1,0:T(8,128)(2,1)}) %all-gather.5.cloned.1.call-update) | async-done | bytes 4194320 | tf_op jit(solution)/shard_map/all_gather | solution.py:97
  217.9 6.3 %copy.56 = bf16[1024,2048]{0,1:T(8,128)(2,1)} copy(bf16[1024,2048]{1,0:T(8,128)(2,1)} %all-gather.5.cloned.1.call-done) | data formatting | bytes 8388608 | tf_op jit(solution)/shard_map/all_gather | solution.py:97
  224.2 7.6 %fusion.4 = f32[16,192,128]{2,1,0:T(8,128)S(1)} fusion(bf16[1024,16,128]{0,2,1:T(8,128)(2,1)} %bitcast.70, f32[16,192,1024]{2,1,0:T(8,128)} %copy-done.2, f32[16,192]{1,0:T(8,128)S(1)} %get-tuple-element.23, pred[192,1024]{1,0:T(8,128)(4,1)S(1)} %broadcast_compare_fusion), kind=kOutput, calls=%fused_computation.8 | convolution fusion | flops 817889280 | bytes 18558976 | tf_op jit(solution)/shard_map/hqk,khd->hqd/dot_general | solution.py:51
  231.8 0.0 collective-permute-done.2
  231.9 0.0 collective-permute-done.3
  231.9 5.8 %fusion.42 = bf16[16,24,8,128]{3,2,1,0:T(8,128)(2,1)S(1)} fusion(f32[16,192,128]{2,1,0:T(8,128)S(1)} %fusion.4, bf16[192,16,128]{2,0,1:T(8,128)(2,1)S(1)} %copy_bitcast_fusion, bf16[192,16,128]{2,0,1:T(8,128)(2,1)} %collective-permute-done.3, bf16[192,16,128]{2,0,1:T(8,128)(2,1)} %collective-permute-done.2, f32[16,192,576]{2,1,0:T(8,128)} %get-tuple-element.29, ...), kind=kOutput, calls=%fused_computation.49 | convolution fusion | flops 469106688 | bytes 11956224 | tf_op jit(solution)/shard_map/hqk,khd->hqd/dot_general | solution.py:51
  237.7 0.0 copy-start.1
  237.7 10.6 %convolution_convert_fusion = bf16[192,4096]{1,0:T(8,128)(2,1)} fusion(bf16[2048,4096]{1,0:T(8,128)(2,1)} %param.15, bf16[16,24,8,128]{3,2,1,0:T(8,128)(2,1)S(1)} %fusion.42), kind=kOutput, calls=%fused_computation.15 | convolution fusion | flops 3222011904 | bytes 19136512 | tf_op jit(solution)/shard_map/dot_general | solution.py:111
  248.3 0.0 reduce-scatter.2.cloned.1.call-update
  248.3 7.8 %reduce-scatter.2.cloned.1.call-done = bf16[192,2048]{1,0:T(8,128)(2,1)} async-done(((bf16[192,4096]{1,0:T(8,128)(2,1)}), bf16[192,2048]{1,0:T(8,128)(2,1)}) %reduce-scatter.2.cloned.1.call-update) | async-done | bytes 786448 | tf_op jit(solution)/shard_map/reduce_scatter | solution.py:112
  (22 shorter events, 0.1 us)
Async XLA Ops:
  6.5 4.2 %copy-start = (bf16[192,2048]{1,0:T(8,128)(2,1)S(1)}, bf16[192,2048]{1,0:T(8,128)(2,1)}, u32[]{:S(2)}) copy-start(bf16[192,2048]{1,0:T(8,128)(2,1)} %param.9) | copy-start | bytes 2359300
  6.5 4.8 %copy-start.4 = (bf16[192,2048]{1,0:T(8,128)(2,1)S(1)}, bf16[192,2048]{1,0:T(8,128)(2,1)}, u32[]{:S(2)}) copy-start(bf16[192,2048]{1,0:T(8,128)(2,1)} %param.8) | copy-start | bytes 2359300
  6.5 135.6 %all-gather.3.cloned.1.call-start = ((), (), s32[]{:S(2)}) async-start(), calls=%async_computation.1 | async-start | bytes 4456448 | tf_op jit(solution)/shard_map/all_gather | solution.py:96
  7.3 210.7 %all-gather.5.cloned.1.call-start = ((), (), s32[]{:S(2)}) async-start(), calls=%async_computation.2 | async-start | bytes 4456448 | tf_op jit(solution)/shard_map/all_gather | solution.py:97
  8.0 248.1 %reduce-scatter.2.cloned.1.call-start = ((), (), s32[]{:S(2)}) async-start(), calls=%async_computation.3 | async-start | bytes 2359296 | tf_op jit(solution)/shard_map/reduce_scatter | solution.py:112
  12.8 9.8 %copy-start.3 = (bf16[192,2048]{1,0:T(8,128)(2,1)S(1)}, bf16[192,2048]{1,0:T(8,128)(2,1)}, u32[]{:S(2)}) copy-start(bf16[192,2048]{1,0:T(8,128)(2,1)} %param.10) | copy-start | bytes 2359300
  14.3 58.4 %collective-permute-start = (bf16[192,16,128]{2,0,1:T(8,128)(2,1)S(1)}, bf16[192,16,128]{2,0,1:T(8,128)(2,1)S(1)}, u32[]{:S(2)}, u32[]{:S(2)}) collective-permute-start(bf16[192,16,128]{2,0,1:T(8,128)(2,1)S(1)} %pad_maximum_fusion.1), channel_id=1, source_target_pairs={{0,2},{1,3},{2,4},{3,5},{4,6},{5,7},{6,8},{7,9},{8,10},{9,11},{10,... | collective-permute-start | bytes 2359304 | tf_op jit(solution)/shard_map/ppermute | solution.py:16
  19.2 53.5 %collective-permute-start.1 = (bf16[192,16,128]{2,0,1:T(8,128)(2,1)S(1)}, bf16[192,16,128]{2,0,1:T(8,128)(2,1)S(1)}, u32[]{:S(2)}, u32[]{:S(2)}) collective-permute-start(bf16[192,16,128]{2,0,1:T(8,128)(2,1)S(1)} %pad_maximum_fusion.1), channel_id=1, source_target_pairs={{0,1},{1,2},{2,3},{3,4},{4,5},{5,6},{6,7},{7,8},{8,9},{9,10},{10,1... | collective-permute-start | bytes 2359304 | tf_op jit(solution)/shard_map/ppermute | solution.py:16
  22.9 209.0 %collective-permute-start.2 = (bf16[192,16,128]{2,0,1:T(8,128)(2,1)S(1)}, bf16[192,16,128]{2,0,1:T(8,128)(2,1)}, u32[]{:S(2)}, u32[]{:S(2)}) collective-permute-start(bf16[192,16,128]{2,0,1:T(8,128)(2,1)S(1)} %copy_bitcast_fusion), channel_id=1, source_target_pairs={{0,2},{1,3},{2,4},{3,5},{4,6},{5,7},{6,8},{7,9},{8,10},{9,11},{10,... | collective-permute-start | bytes 2359304 | tf_op jit(solution)/shard_map/ppermute | solution.py:16
  27.1 204.7 %collective-permute-start.3 = (bf16[192,16,128]{2,0,1:T(8,128)(2,1)S(1)}, bf16[192,16,128]{2,0,1:T(8,128)(2,1)}, u32[]{:S(2)}, u32[]{:S(2)}) collective-permute-start(bf16[192,16,128]{2,0,1:T(8,128)(2,1)S(1)} %copy_bitcast_fusion), channel_id=1, source_target_pairs={{0,1},{1,2},{2,3},{3,4},{4,5},{5,6},{6,7},{7,8},{8,9},{9,10},{10,1... | collective-permute-start | bytes 2359304 | tf_op jit(solution)/shard_map/ppermute | solution.py:16
  148.6 5.2 %slice-start = ((s8[7864320]{0:T(1024)(128)(4,1)}), s8[4194304]{0:T(1024)(128)(4,1)S(1)}, s32[]{:S(2)}) async-start(s8[7864320]{0:T(1024)(128)(4,1)} %bitcast.68), calls=%async_computation.4 | async-start | bytes 8388608
  148.6 5.2 %slice-start.1 = ((s8[7864320]{0:T(1024)(128)(4,1)}), s8[3670016]{0:T(1024)(128)(4,1)S(1)}, s32[]{:S(2)}) async-start(s8[7864320]{0:T(1024)(128)(4,1)} %bitcast.68), calls=%async_computation.5 | async-start | bytes 7340032
  153.8 6.0 %copy-start.2 = (f32[16,192,1024]{2,1,0:T(8,128)}, f32[16,192,1024]{2,1,0:T(8,128)S(1)}, u32[]{:S(2)}) copy-start(f32[16,192,1024]{2,1,0:T(8,128)S(1)} %get-tuple-element.31) | copy-start | bytes 37748740
  237.7 18.5 %copy-start.1 = (bf16[192,2048]{1,0:T(8,128)(2,1)S(1)}, bf16[192,2048]{1,0:T(8,128)(2,1)}, u32[]{:S(2)}) copy-start(bf16[192,2048]{1,0:T(8,128)(2,1)} %param.9) | copy-start | bytes 2359300
Sparse Core Ops, SparseCore 0:
  10.1 131.9 all-gather.2
  144.9 72.9 all-gather.4
  248.4 7.6 reduce-scatter.1
where the time goes:
time: 263 us
  waiting for transfers between devices  172 us (65%)
  matrix products  34 us (13%)
  starting transfers between devices  17 us (6%)
  local copies, waits for them, and re-layouts  14.5 us (6%)
  between operations  13.4 us (5%)
  other arithmetic  11.3 us (4%)
    all_gather x1, waiting for transfers between devices, body(): piece_k = lax.all_gather(prefix_keys, 'blk', axis=0, tiled=True)  64.7 us
    all_gather x1, waiting for transfers between devices, body(): piece_v = lax.all_gather(prefix_values, 'blk', axis=0, tiled=True)  58.2 us
    ppermute x4, waiting for transfers between devices, shifted(): return lax.ppermute(block, axis, route)  40.4 us
    ppermute x4, starting transfers between devices, shifted(): return lax.ppermute(block, axis, route)  16.9 us
    dot_general x2, matrix products, online_update(): jnp.einsum('hqk,khd->hqd', weights, value_rows, preferred_element_type=jn...  13.4 us
    dot_general x1, matrix products, body(): partial_out = jnp.dot(attn, out_weight, preferred_element_type=jnp.float32)  10.6 us
    dot_general x2, matrix products, online_update(): jnp.einsum('qhd,khd->hqk', q_rot, key_rows, preferred_element_type=jnp.fl...  9.99 us
    reduce_scatter x1, waiting for transfers between devices, body(): lax.psum_scatter(partial_out.astype(jnp.bfloat16), 'heads', scatter_dimen...  7.82 us
  transfers between devices with their start and end apart: 7, of which 4 were waited for; matrix products, arithmetic and copies ran while one was open for 17% of the time, Pallas kernels for 0%

commit v1 on v0

--- a/solution.py
+++ b/solution.py
@@ -8,6 +8,19 @@
 ROT = 32
 GROUPS = 4
 MOST = 224
+
+
+def ring_gather(value, axis, dim):
+    ways = lax.axis_size(axis)
+    up = [(d, (d + 1) % ways) for d in range(ways)]
+    down = [(d, (d - 1) % ways) for d in range(ways)]
+    earlier, later = ([value], [value])
+    for _ in range(ways // 2):
+        earlier.append(lax.ppermute(earlier[-1], axis, up))
+    for _ in range((ways - 1) // 2):
+        later.append(lax.ppermute(later[-1], axis, down))
+    line = jnp.concatenate([*earlier[::-1], *later[1:]], axis=dim)
+    return jnp.roll(line, (lax.axis_index(axis) - ways // 2) * value.shape[dim], axis=dim)
 
 
 def shifted(block, axis, distance):
@@ -93,7 +106,7 @@
         jnp.zeros((heads_dev, tok, HD), jnp.float32),
     )
     state = online_update(state, q_rot, near_k, near_v, near_mask, scale)
-    piece_k = lax.all_gather(prefix_keys, "blk", axis=0, tiled=True)
+    piece_k = ring_gather(prefix_keys, "blk", 0)
     piece_v = lax.all_gather(prefix_values, "blk", axis=0, tiled=True)
     count = piece_k.shape[0]
     row_group = jnp.arange(count, dtype=jnp.int32) // prefix_len

time: 263 us -> 355 us (1.35)
  starting transfers between devices: 17 us -> 95.4 us
  local copies, waits for them, and re-layouts: 14.5 us -> 38.4 us
  waiting for transfers between devices: 172 us -> 157 us
    ppermute x0 -> x15, waiting for transfers between devices: none -> 131 us  [the longest x8 86.2 us: ring_gather(): earlier.append(lax.ppermute(earlier[-1], axis, up))]
    ppermute x0 -> x15, starting transfers between devices: none -> 65.3 us  [the longest x7 46.3 us: ring_gather(): later.append(lax.ppermute(later[-1], axis, down))]
    all_gather x1 -> x0, waiting for transfers between devices: 64.7 us -> none  [body(): piece_k = lax.all_gather(prefix_keys, 'blk', axis=0, tiled=True)]
    all_gather x1, waiting for transfers between devices: 58.2 us -> 0.02 us  [body(): piece_v = lax.all_gather(prefix_values, 'blk', axis=0, tiled=True)]
    ppermute x4, waiting for transfers between devices: 40.4 us -> 0.01 us  [shifted(): return lax.ppermute(block, axis, route)]
    concatenate x0 -> x1, local copies, waits for them, and re-layouts: none -> 20.6 us  [ring_gather(): jnp.roll(line, (lax.axis_index(axis) - ways // 2) * value.shape[dim], axi...]
    reduce_scatter x1, waiting for transfers between devices: 7.82 us -> 25.5 us  [body(): lax.psum_scatter(partial_out.astype(jnp.bfloat16), 'heads', scatter_dimen...]
    ppermute x4, starting transfers between devices: 16.9 us -> 30.1 us  [shifted(): return lax.ppermute(block, axis, route)]
  transfers between devices with their start and end apart: 7 -> 21, of which waited for: 4 -> 11; matrix products, arithmetic and copies ran while one was open for 17% -> 19% of each run, Pallas kernels for 0% -> 0%
where the time goes in v1:
time: 355 us; the launch traced here: 353 us
  waiting for transfers between devices  157 us (44%)
  starting transfers between devices  95.4 us (27%)
  local copies, waits for them, and re-layouts  38.4 us (11%)
  matrix products  34.5 us (10%)
  other arithmetic  14.1 us (4%)
  between operations  13.7 us (4%)
    ppermute x8, waiting for transfers between devices, ring_gather(): earlier.append(lax.ppermute(earlier[-1], axis, up))  86.2 us
    ppermute x7, starting transfers between devices, ring_gather(): later.append(lax.ppermute(later[-1], axis, down))  46.3 us
    ppermute x7, waiting for transfers between devices, ring_gather(): later.append(lax.ppermute(later[-1], axis, down))  44.5 us
    ppermute x4, starting transfers between devices, shifted(): return lax.ppermute(block, axis, route)  30.1 us
    reduce_scatter x1, waiting for transfers between devices, body(): lax.psum_scatter(partial_out.astype(jnp.bfloat16), 'heads', scatter_dimen...  25.5 us
    concatenate x1, local copies, waits for them, and re-layouts, ring_gather(): jnp.roll(line, (lax.axis_index(axis) - ways // 2) * value.shape[dim], axi...  20.6 us
    ppermute x8, starting transfers between devices, ring_gather(): earlier.append(lax.ppermute(earlier[-1], axis, up))  18.9 us
    dot_general x2, matrix products, online_update(): jnp.einsum('hqk,khd->hqd', weights, value_rows, preferred_element_type=jn...  13.5 us
  transfers between devices with their start and end apart: 21, of which 11 were waited for; matrix products, arithmetic and copies ran while one was open for 19% of the time, Pallas kernels for 0%

profile of v1, /device:TPU:0, one launch (start us, length us, event | category | flops | bytes accessed | tf_op | source)
XLA Modules:
  0.0 353.0 jit_solution(1478865864723497147)
XLA Ops:
  6.5 0.7 all-gather.2.cloned.1.call-update
  7.3 1.2 copy.60
  8.5 3.0 collective-permute-start.4
  11.5 4.1 %collective-permute-start.12 = (bf16[64,2048]{0,1:T(8,128)(2,1)S(1)}, bf16[64,2048]{0,1:T(8,128)(2,1)S(1)}, u32[]{:S(2)}, u32[]{:S(2)}) collective-permute-start(bf16[64,2048]{0,1:T(8,128)(2,1)S(1)} %copy.60), channel_id=1, source_target_pairs={{0,15},{1,0},{2,1},{3,2},{4,3},{5,4},{6,5},{7,6},{8,7},{9,8},{10,9... | collective-permute-start | bytes 786440 | tf_op jit(solution)/shard_map/ppermute | solution.py:21
  15.6 0.7 copy.50
  16.5 0.7 broadcast_add_fusion.2
  17.2 0.7 select_reduce_fusion.1
  18.6 1.4 fusion.69
  20.0 15.8 %collective-permute-done.4 = bf16[64,2048]{0,1:T(8,128)(2,1)S(1)} collective-permute-done((bf16[64,2048]{0,1:T(8,128)(2,1)S(1)}, bf16[64,2048]{0,1:T(8,128)(2,1)S(1)}, u32[]{:S(2)}, u32[]{:S(2)}) %collective-permute-start.4) | collective-permute-done | bytes 262176 | tf_op jit(solution)/shard_map/ppermute | solution.py:19
  35.8 2.5 collective-permute-start.5
  38.3 1.1 slice_negate_fusion
  39.5 3.2 collective-permute-start.13
  42.7 25.4 %collective-permute-done.5 = bf16[64,2048]{0,1:T(8,128)(2,1)S(1)} collective-permute-done((bf16[64,2048]{0,1:T(8,128)(2,1)S(1)}, bf16[64,2048]{0,1:T(8,128)(2,1)S(1)}, u32[]{:S(2)}, u32[]{:S(2)}) %collective-permute-start.5) | collective-permute-done | bytes 262176 | tf_op jit(solution)/shard_map/ppermute | solution.py:19
  68.1 2.5 collective-permute-start.6
  70.6 1.8 fusion.32
  72.7 0.6 copy-done.3
  73.3 1.3 pad_maximum_fusion.1
  74.6 2.2 collective-permute-start
  76.8 5.4 %collective-permute-start.1 = (bf16[192,16,128]{2,0,1:T(8,128)(2,1)}, bf16[192,16,128]{2,0,1:T(8,128)(2,1)}, u32[]{:S(2)}, u32[]{:S(2)}) collective-permute-start(bf16[192,16,128]{2,0,1:T(8,128)(2,1)} %pad_maximum_fusion.1), channel_id=1, source_target_pairs={{0,1},{1,2},{2,3},{3,4},{4,5},{5,6},{6,7},{7,8},{8,9},{9,10},{10,1... | collective-permute-start | bytes 2359304 | tf_op jit(solution)/shard_map/ppermute | solution.py:29
  82.2 1.4 collective-permute-done.6
  83.7 3.2 collective-permute-start.7
  86.8 1.1 copy_bitcast_fusion
  87.9 2.2 collective-permute-start.2
  90.1 35.5 %collective-permute-done.14 = bf16[64,2048]{0,1:T(8,128)(2,1)S(1)} collective-permute-done((bf16[64,2048]{0,1:T(8,128)(2,1)S(1)}, bf16[64,2048]{0,1:T(8,128)(2,1)S(1)}, u32[]{:S(2)}, u32[]{:S(2)}) %collective-permute-start.14) | collective-permute-done | bytes 262176 | tf_op jit(solution)/shard_map/ppermute | solution.py:21
  125.7 18.5 %collective-permute-done.7 = bf16[64,2048]{0,1:T(8,128)(2,1)S(1)} collective-permute-done((bf16[64,2048]{0,1:T(8,128)(2,1)S(1)}, bf16[64,2048]{0,1:T(8,128)(2,1)S(1)}, u32[]{:S(2)}, u32[]{:S(2)}) %collective-permute-start.7) | collective-permute-done | bytes 262176 | tf_op jit(solution)/shard_map/ppermute | solution.py:19
  144.1 2.5 collective-permute-start.8
  146.8 5.0 %collective-permute-start.16 = (bf16[64,2048]{0,1:T(8,128)(2,1)S(1)}, bf16[64,2048]{0,1:T(8,128)(2,1)}, u32[]{:S(2)}, u32[]{:S(2)}) collective-permute-start(bf16[64,2048]{0,1:T(8,128)(2,1)S(1)} %collective-permute-done.15), channel_id=1, source_target_pairs={{0,15},{1,0},{2,1},{3,2},{4,3},{5,4},{6,5},{7,6},{8,7},{9,8},{10,9... | collective-permute-start | bytes 786440 | tf_op jit(solution)/shard_map/ppermute | solution.py:21
  151.8 11.0 %collective-permute-done.8 = bf16[64,2048]{0,1:T(8,128)(2,1)S(1)} collective-permute-done((bf16[64,2048]{0,1:T(8,128)(2,1)S(1)}, bf16[64,2048]{0,1:T(8,128)(2,1)S(1)}, u32[]{:S(2)}, u32[]{:S(2)}) %collective-permute-start.8) | collective-permute-done | bytes 262176 | tf_op jit(solution)/shard_map/ppermute | solution.py:19
  162.8 2.8 collective-permute-start.9
  165.7 5.1 %collective-permute-done.16 = bf16[64,2048]{0,1:T(8,128)(2,1)} collective-permute-done((bf16[64,2048]{0,1:T(8,128)(2,1)S(1)}, bf16[64,2048]{0,1:T(8,128)(2,1)}, u32[]{:S(2)}, u32[]{:S(2)}) %collective-permute-start.16) | collective-permute-done | bytes 262176 | tf_op jit(solution)/shard_map/ppermute | solution.py:21
  170.8 8.2 %collective-permute-done.9 = bf16[64,2048]{0,1:T(8,128)(2,1)} collective-permute-done((bf16[64,2048]{0,1:T(8,128)(2,1)S(1)}, bf16[64,2048]{0,1:T(8,128)(2,1)}, u32[]{:S(2)}, u32[]{:S(2)}) %collective-permute-start.9) | collective-permute-done | bytes 262176 | tf_op jit(solution)/shard_map/ppermute | solution.py:19
  179.0 2.6 collective-permute-start.10
  182.1 20.2 %collective-permute-start.3 = (bf16[192,16,128]{2,0,1:T(8,128)(2,1)}, bf16[192,16,128]{2,0,1:T(8,128)(2,1)}, u32[]{:S(2)}, u32[]{:S(2)}) collective-permute-start(bf16[192,16,128]{2,0,1:T(8,128)(2,1)} %copy_bitcast_fusion), channel_id=1, source_target_pairs={{0,1},{1,2},{2,3},{3,4},{4,5},{5,6},{6,7},{7,8},{8,9},{9,10},{10,1... | collective-permute-start | bytes 2359304 | tf_op jit(solution)/shard_map/ppermute | solution.py:29
  202.3 34.1 %collective-permute-start.18 = (bf16[64,2048]{0,1:T(8,128)(2,1)}, bf16[64,2048]{0,1:T(8,128)(2,1)}, u32[]{:S(2)}, u32[]{:S(2)}) collective-permute-start(bf16[64,2048]{0,1:T(8,128)(2,1)} %collective-permute-done.17), channel_id=1, source_target_pairs={{0,15},{1,0},{2,1},{3,2},{4,3},{5,4},{6,5},{7,6},{8,7},{9,8},{10,9... | collective-permute-start | bytes 786440 | tf_op jit(solution)/shard_map/ppermute | solution.py:21
  236.5 7.4 %fusion.3 = (f32[16,192]{1,0:T(8,128)S(1)}, f32[16,192,576]{2,1,0:T(8,128)}) fusion(pred[192,576]{1,0:T(8,128)(4,1)S(1)} %compare_and_fusion, bf16[192,16,96]{2,0,1:T(8,128)(2,1)S(1)} %slice.45, bf16[192,16,32]{2,0,1:T(8,128)(2,1)} %copy-done.3, bf16[192,16,128]{2,0,1:T(8,128)(2,1)} %collective-permute-done.1, ...), kind=kOutput, calls=%fused_computation.7 | convolution fusion | flops 469300224 | bytes 10346496 | tf_op jit(solution)/shard_map/qhd,khd->hqk/dot_general | solution.py:57
  243.8 3.9 %collective-permute-done.18 = bf16[64,2048]{0,1:T(8,128)(2,1)} collective-permute-done((bf16[64,2048]{0,1:T(8,128)(2,1)}, bf16[64,2048]{0,1:T(8,128)(2,1)}, u32[]{:S(2)}, u32[]{:S(2)}) %collective-permute-start.18) | collective-permute-done | bytes 262176 | tf_op jit(solution)/shard_map/ppermute | solution.py:21
  247.7 5.8 %collective-permute-done.11 = bf16[64,2048]{0,1:T(8,128)(2,1)} collective-permute-done((bf16[64,2048]{0,1:T(8,128)(2,1)}, bf16[64,2048]{0,1:T(8,128)(2,1)}, u32[]{:S(2)}, u32[]{:S(2)}) %collective-permute-start.11) | collective-permute-done | bytes 262176 | tf_op jit(solution)/shard_map/ppermute | solution.py:19
  253.5 20.6 %concatenate.49 = bf16[2048,2048]{0,1:T(8,128)(2,1)} concatenate(bf16[64,2048]{0,1:T(8,128)(2,1)} %collective-permute-done.11, bf16[64,2048]{0,1:T(8,128)(2,1)} %collective-permute-done.10, bf16[64,2048]{0,1:T(8,128)(2,1)} %collective-permute-done.9, bf16[64,2048]{0,1:T(8,128)(2,1)} %copy-done.13, bf16[64,2048]{0,1:T(8,128)(2,1)} %copy-done.11, bf16[64,2048]{0,1:T(8,128)(2,1)} %copy-done.9, ...), dimensions={0} | concatenate | bytes 16777216 | tf_op jit(solution)/shard_map/jit(_roll_dynamic)/concatenate | solution.py:23
  274.2 4.6 %constant_dynamic-slice_fusion = bf16[1024,2048]{0,1:T(8,128)(2,1)S(1)} fusion(bf16[2048,2048]{0,1:T(8,128)(2,1)} %concatenate.49, s32[]{:T(128)S(6)} %select_n.47), kind=kLoop, calls=%fused_computation.93 | loop fusion | bytes 8388612 | tf_op jit(solution)/shard_map/jit(_roll_dynamic)/dynamic_slice | solution.py:23
  278.8 3.2 fusion
  282.1 2.3 fusion.10
  284.4 2.2 copy-done.2
  286.6 3.6 %fusion.1 = f32[16,192]{1,0:T(8,128)S(1)} fusion(f32[16,192,1024]{2,1,0:T(8,128)S(1)} %get-tuple-element.31, f32[16,192]{1,0:T(8,128)S(1)} %get-tuple-element.23, pred[192,1024]{1,0:T(8,128)(4,1)S(1)} %broadcast_compare_fusion), kind=kLoop, calls=%fused_computation.3 | loop fusion | flops 12579840 | bytes 12804096 | tf_op jit(solution)/shard_map/reduce_sum | solution.py:62
  290.2 6.4 %copy.65 = bf16[1024,2048]{0,1:T(8,128)(2,1)} copy(bf16[1024,2048]{1,0:T(8,128)(2,1)} %all-gather.2.cloned.1.call-done) | data formatting | bytes 8388608 | tf_op jit(solution)/shard_map/all_gather | solution.py:110
  296.6 7.6 %fusion.4 = f32[16,192,128]{2,1,0:T(8,128)S(1)} fusion(bf16[1024,16,128]{0,2,1:T(8,128)(2,1)} %bitcast.70, f32[16,192,1024]{2,1,0:T(8,128)} %copy-done.2, f32[16,192]{1,0:T(8,128)S(1)} %get-tuple-element.23, pred[192,1024]{1,0:T(8,128)(4,1)S(1)} %broadcast_compare_fusion), kind=kOutput, calls=%fused_computation.8 | convolution fusion | flops 817889280 | bytes 18558976 | tf_op jit(solution)/shard_map/hqk,khd->hqd/dot_general | solution.py:64
  304.3 5.9 %fusion.42 = bf16[16,24,8,128]{3,2,1,0:T(8,128)(2,1)S(1)} fusion(f32[16,192,128]{2,1,0:T(8,128)S(1)} %fusion.4, bf16[192,16,128]{2,0,1:T(8,128)(2,1)} %copy_bitcast_fusion, bf16[192,16,128]{2,0,1:T(8,128)(2,1)} %collective-permute-done.3, bf16[192,16,128]{2,0,1:T(8,128)(2,1)} %collective-permute-done.2, f32[16,192,576]{2,1,0:T(8,128)} %get-tuple-element.29, ...), kind=kOutput, calls=%fused_computation.49 | convolution fusion | flops 469106688 | bytes 11956224 | tf_op jit(solution)/shard_map/hqk,khd->hqd/dot_general | solution.py:64
  310.2 10.4 %convolution_convert_fusion = bf16[192,4096]{1,0:T(8,128)(2,1)} fusion(bf16[2048,4096]{1,0:T(8,128)(2,1)} %param.15, bf16[16,24,8,128]{3,2,1,0:T(8,128)(2,1)S(1)} %fusion.42), kind=kOutput, calls=%fused_computation.15 | convolution fusion | flops 3222011904 | bytes 19136512 | tf_op jit(solution)/shard_map/dot_general | solution.py:124
  320.7 25.5 %reduce-scatter.2.cloned.1.call-done = bf16[192,2048]{1,0:T(8,128)(2,1)} async-done(((bf16[192,4096]{1,0:T(8,128)(2,1)}), bf16[192,2048]{1,0:T(8,128)(2,1)}) %reduce-scatter.2.cloned.1.call-update) | async-done | bytes 786448 | tf_op jit(solution)/shard_map/reduce_scatter | solution.py:125
  (71 shorter events, 2.2 us)
Async XLA Ops:
  6.5 11.8 %copy-start = (bf16[192,2048]{1,0:T(8,128)(2,1)S(1)}, bf16[192,2048]{1,0:T(8,128)(2,1)}, u32[]{:S(2)}) copy-start(bf16[192,2048]{1,0:T(8,128)(2,1)} %param.9) | copy-start | bytes 2359300
  6.5 283.7 %all-gather.2.cloned.1.call-start = ((), (), s32[]{:S(2)}) async-start(), calls=%async_computation.1 | async-start | bytes 4456448 | tf_op jit(solution)/shard_map/all_gather | solution.py:110
  7.3 338.9 %reduce-scatter.2.cloned.1.call-start = ((), (), s32[]{:S(2)}) async-start(), calls=%async_computation.2 | async-start | bytes 2359296 | tf_op jit(solution)/shard_map/reduce_scatter | solution.py:125
  8.5 27.3 %collective-permute-start.4 = (bf16[64,2048]{0,1:T(8,128)(2,1)S(1)}, bf16[64,2048]{0,1:T(8,128)(2,1)S(1)}, u32[]{:S(2)}, u32[]{:S(2)}) collective-permute-start(bf16[64,2048]{0,1:T(8,128)(2,1)S(1)} %copy.60), channel_id=1, source_target_pairs={{0,1},{1,2},{2,3},{3,4},{4,5},{5,6},{6,7},{7,8},{8,9},{9,10},{10,1... | collective-permute-start | bytes 786440 | tf_op jit(solution)/shard_map/ppermute | solution.py:19
  11.5 27.9 %collective-permute-start.12 = (bf16[64,2048]{0,1:T(8,128)(2,1)S(1)}, bf16[64,2048]{0,1:T(8,128)(2,1)S(1)}, u32[]{:S(2)}, u32[]{:S(2)}) collective-permute-start(bf16[64,2048]{0,1:T(8,128)(2,1)S(1)} %copy.60), channel_id=1, source_target_pairs={{0,15},{1,0},{2,1},{3,2},{4,3},{5,4},{6,5},{7,6},{8,7},{9,8},{10,9... | collective-permute-start | bytes 786440 | tf_op jit(solution)/shard_map/ppermute | solution.py:21
  35.8 32.3 %collective-permute-start.5 = (bf16[64,2048]{0,1:T(8,128)(2,1)S(1)}, bf16[64,2048]{0,1:T(8,128)(2,1)S(1)}, u32[]{:S(2)}, u32[]{:S(2)}) collective-permute-start(bf16[64,2048]{0,1:T(8,128)(2,1)S(1)} %collective-permute-done.4), channel_id=1, source_target_pairs={{0,1},{1,2},{2,3},{3,4},{4,5},{5,6},{6,7},{7,8},{8,9},{9,10},{10,1... | collective-permute-start | bytes 786440 | tf_op jit(solution)/shard_map/ppermute | solution.py:19
  39.5 32.9 %copy-start.5 = (bf16[64,2048]{0,1:T(8,128)(2,1)}, bf16[64,2048]{0,1:T(8,128)(2,1)S(1)}, u32[]{:S(2)}) copy-start(bf16[64,2048]{0,1:T(8,128)(2,1)S(1)} %collective-permute-done.12) | copy-start | bytes 786436
  39.5 42.7 %collective-permute-start.13 = (bf16[64,2048]{0,1:T(8,128)(2,1)S(1)}, bf16[64,2048]{0,1:T(8,128)(2,1)S(1)}, u32[]{:S(2)}, u32[]{:S(2)}) collective-permute-start(bf16[64,2048]{0,1:T(8,128)(2,1)S(1)} %collective-permute-done.12), channel_id=1, source_target_pairs={{0,15},{1,0},{2,1},{3,2},{4,3},{5,4},{6,5},{7,6},{8,7},{9,8},{10,9... | collective-permute-start | bytes 786440 | tf_op jit(solution)/shard_map/ppermute | solution.py:21
  68.1 4.3 %copy-start.7 = (bf16[64,2048]{0,1:T(8,128)(2,1)}, bf16[64,2048]{0,1:T(8,128)(2,1)S(1)}, u32[]{:S(2)}) copy-start(bf16[64,2048]{0,1:T(8,128)(2,1)S(1)} %collective-permute-done.5) | copy-start | bytes 786436
  68.1 15.5 %collective-permute-start.6 = (bf16[64,2048]{0,1:T(8,128)(2,1)S(1)}, bf16[64,2048]{0,1:T(8,128)(2,1)S(1)}, u32[]{:S(2)}, u32[]{:S(2)}) collective-permute-start(bf16[64,2048]{0,1:T(8,128)(2,1)S(1)} %collective-permute-done.5), channel_id=1, source_target_pairs={{0,1},{1,2},{2,3},{3,4},{4,5},{5,6},{6,7},{7,8},{8,9},{9,10},{10,1... | collective-permute-start | bytes 786440 | tf_op jit(solution)/shard_map/ppermute | solution.py:19
  72.4 0.9 copy-start.3
  72.4 14.4 %copy-start.14 = (bf16[192,2048]{1,0:T(8,128)(2,1)S(1)}, bf16[192,2048]{1,0:T(8,128)(2,1)}, u32[]{:S(2)}) copy-start(bf16[192,2048]{1,0:T(8,128)(2,1)} %param.10) | copy-start | bytes 2359300
  74.6 107.5 %collective-permute-start = (bf16[192,16,128]{2,0,1:T(8,128)(2,1)}, bf16[192,16,128]{2,0,1:T(8,128)(2,1)}, u32[]{:S(2)}, u32[]{:S(2)}) collective-permute-start(bf16[192,16,128]{2,0,1:T(8,128)(2,1)} %pad_maximum_fusion.1), channel_id=1, source_target_pairs={{0,2},{1,3},{2,4},{3,5},{4,6},{5,7},{6,8},{7,9},{8,10},{9,11},{10,... | collective-permute-start | bytes 2359304 | tf_op jit(solution)/shard_map/ppermute | solution.py:29
  76.8 159.7 %collective-permute-start.1 = (bf16[192,16,128]{2,0,1:T(8,128)(2,1)}, bf16[192,16,128]{2,0,1:T(8,128)(2,1)}, u32[]{:S(2)}, u32[]{:S(2)}) collective-permute-start(bf16[192,16,128]{2,0,1:T(8,128)(2,1)} %pad_maximum_fusion.1), channel_id=1, source_target_pairs={{0,1},{1,2},{2,3},{3,4},{4,5},{5,6},{6,7},{7,8},{8,9},{9,10},{10,1... | collective-permute-start | bytes 2359304 | tf_op jit(solution)/shard_map/ppermute | solution.py:29
  82.2 1.4 copy-start.8
  82.2 43.4 %collective-permute-start.14 = (bf16[64,2048]{0,1:T(8,128)(2,1)S(1)}, bf16[64,2048]{0,1:T(8,128)(2,1)S(1)}, u32[]{:S(2)}, u32[]{:S(2)}) collective-permute-start(bf16[64,2048]{0,1:T(8,128)(2,1)S(1)} %collective-permute-done.13), channel_id=1, source_target_pairs={{0,15},{1,0},{2,1},{3,2},{4,3},{5,4},{6,5},{7,6},{8,7},{9,8},{10,9... | collective-permute-start | bytes 786440 | tf_op jit(solution)/shard_map/ppermute | solution.py:21
  83.6 42.0 %copy-start.9 = (bf16[64,2048]{0,1:T(8,128)(2,1)}, bf16[64,2048]{0,1:T(8,128)(2,1)S(1)}, u32[]{:S(2)}) copy-start(bf16[64,2048]{0,1:T(8,128)(2,1)S(1)} %collective-permute-done.6) | copy-start | bytes 786436
  83.7 60.5 %collective-permute-start.7 = (bf16[64,2048]{0,1:T(8,128)(2,1)S(1)}, bf16[64,2048]{0,1:T(8,128)(2,1)S(1)}, u32[]{:S(2)}, u32[]{:S(2)}) collective-permute-start(bf16[64,2048]{0,1:T(8,128)(2,1)S(1)} %collective-permute-done.6), channel_id=1, source_target_pairs={{0,1},{1,2},{2,3},{3,4},{4,5},{5,6},{6,7},{7,8},{8,9},{9,10},{10,1... | collective-permute-start | bytes 786440 | tf_op jit(solution)/shard_map/ppermute | solution.py:19
  87.9 216.3 %collective-permute-start.2 = (bf16[192,16,128]{2,0,1:T(8,128)(2,1)}, bf16[192,16,128]{2,0,1:T(8,128)(2,1)}, u32[]{:S(2)}, u32[]{:S(2)}) collective-permute-start(bf16[192,16,128]{2,0,1:T(8,128)(2,1)} %copy_bitcast_fusion), channel_id=1, source_target_pairs={{0,2},{1,3},{2,4},{3,5},{4,6},{5,7},{6,8},{7,9},{8,10},{9,11},{10,... | collective-permute-start | bytes 2359304 | tf_op jit(solution)/shard_map/ppermute | solution.py:29
  125.7 55.9 %copy-start.10 = (bf16[64,2048]{0,1:T(8,128)(2,1)}, bf16[64,2048]{0,1:T(8,128)(2,1)S(1)}, u32[]{:S(2)}) copy-start(bf16[64,2048]{0,1:T(8,128)(2,1)S(1)} %collective-permute-done.14) | copy-start | bytes 786436
  125.7 21.1 %collective-permute-start.15 = (bf16[64,2048]{0,1:T(8,128)(2,1)S(1)}, bf16[64,2048]{0,1:T(8,128)(2,1)S(1)}, u32[]{:S(2)}, u32[]{:S(2)}) collective-permute-start(bf16[64,2048]{0,1:T(8,128)(2,1)S(1)} %collective-permute-done.14), channel_id=1, source_target_pairs={{0,15},{1,0},{2,1},{3,2},{4,3},{5,4},{6,5},{7,6},{8,7},{9,8},{10,9... | collective-permute-start | bytes 786440 | tf_op jit(solution)/shard_map/ppermute | solution.py:21
  144.1 2.7 copy-start.11
  144.1 18.6 %collective-permute-start.8 = (bf16[64,2048]{0,1:T(8,128)(2,1)S(1)}, bf16[64,2048]{0,1:T(8,128)(2,1)S(1)}, u32[]{:S(2)}, u32[]{:S(2)}) collective-permute-start(bf16[64,2048]{0,1:T(8,128)(2,1)S(1)} %collective-permute-done.7), channel_id=1, source_target_pairs={{0,1},{1,2},{2,3},{3,4},{4,5},{5,6},{6,7},{7,8},{8,9},{9,10},{10,1... | collective-permute-start | bytes 786440 | tf_op jit(solution)/shard_map/ppermute | solution.py:19
  146.8 16.0 %copy-start.12 = (bf16[64,2048]{0,1:T(8,128)(2,1)}, bf16[64,2048]{0,1:T(8,128)(2,1)S(1)}, u32[]{:S(2)}) copy-start(bf16[64,2048]{0,1:T(8,128)(2,1)S(1)} %collective-permute-done.15) | copy-start | bytes 786436
  146.8 24.0 %collective-permute-start.16 = (bf16[64,2048]{0,1:T(8,128)(2,1)S(1)}, bf16[64,2048]{0,1:T(8,128)(2,1)}, u32[]{:S(2)}, u32[]{:S(2)}) collective-permute-start(bf16[64,2048]{0,1:T(8,128)(2,1)S(1)} %collective-permute-done.15), channel_id=1, source_target_pairs={{0,15},{1,0},{2,1},{3,2},{4,3},{5,4},{6,5},{7,6},{8,7},{9,8},{10,9... | collective-permute-start | bytes 786440 | tf_op jit(solution)/shard_map/ppermute | solution.py:21
  162.8 8.0 %copy-start.13 = (bf16[64,2048]{0,1:T(8,128)(2,1)}, bf16[64,2048]{0,1:T(8,128)(2,1)S(1)}, u32[]{:S(2)}) copy-start(bf16[64,2048]{0,1:T(8,128)(2,1)S(1)} %collective-permute-done.8) | copy-start | bytes 786436
  162.8 16.2 %collective-permute-start.9 = (bf16[64,2048]{0,1:T(8,128)(2,1)S(1)}, bf16[64,2048]{0,1:T(8,128)(2,1)}, u32[]{:S(2)}, u32[]{:S(2)}) collective-permute-start(bf16[64,2048]{0,1:T(8,128)(2,1)S(1)} %collective-permute-done.8), channel_id=1, source_target_pairs={{0,1},{1,2},{2,3},{3,4},{4,5},{5,6},{6,7},{7,8},{8,9},{9,10},{10,1... | collective-permute-start | bytes 786440 | tf_op jit(solution)/shard_map/ppermute | solution.py:19
  170.8 31.5 %collective-permute-start.17 = (bf16[64,2048]{0,1:T(8,128)(2,1)}, bf16[64,2048]{0,1:T(8,128)(2,1)}, u32[]{:S(2)}, u32[]{:S(2)}) collective-permute-start(bf16[64,2048]{0,1:T(8,128)(2,1)} %collective-permute-done.16), channel_id=1, source_target_pairs={{0,15},{1,0},{2,1},{3,2},{4,3},{5,4},{6,5},{7,6},{8,7},{9,8},{10,9... | collective-permute-start | bytes 786440 | tf_op jit(solution)/shard_map/ppermute | solution.py:21
  179.0 57.4 %collective-permute-start.10 = (bf16[64,2048]{0,1:T(8,128)(2,1)}, bf16[64,2048]{0,1:T(8,128)(2,1)}, u32[]{:S(2)}, u32[]{:S(2)}) collective-permute-start(bf16[64,2048]{0,1:T(8,128)(2,1)} %collective-permute-done.9), channel_id=1, source_target_pairs={{0,1},{1,2},{2,3},{3,4},{4,5},{5,6},{6,7},{7,8},{8,9},{9,10},{10,1... | collective-permute-start | bytes 786440 | tf_op jit(solution)/shard_map/ppermute | solution.py:19
  182.1 122.2 %collective-permute-start.3 = (bf16[192,16,128]{2,0,1:T(8,128)(2,1)}, bf16[192,16,128]{2,0,1:T(8,128)(2,1)}, u32[]{:S(2)}, u32[]{:S(2)}) collective-permute-start(bf16[192,16,128]{2,0,1:T(8,128)(2,1)} %copy_bitcast_fusion), channel_id=1, source_target_pairs={{0,1},{1,2},{2,3},{3,4},{4,5},{5,6},{6,7},{7,8},{8,9},{9,10},{10,1... | collective-permute-start | bytes 2359304 | tf_op jit(solution)/shard_map/ppermute | solution.py:29
  202.3 45.4 %collective-permute-start.18 = (bf16[64,2048]{0,1:T(8,128)(2,1)}, bf16[64,2048]{0,1:T(8,128)(2,1)}, u32[]{:S(2)}, u32[]{:S(2)}) collective-permute-start(bf16[64,2048]{0,1:T(8,128)(2,1)} %collective-permute-done.17), channel_id=1, source_target_pairs={{0,15},{1,0},{2,1},{3,2},{4,3},{5,4},{6,5},{7,6},{8,7},{9,8},{10,9... | collective-permute-start | bytes 786440 | tf_op jit(solution)/shard_map/ppermute | solution.py:21
  236.4 17.1 %collective-permute-start.11 = (bf16[64,2048]{0,1:T(8,128)(2,1)}, bf16[64,2048]{0,1:T(8,128)(2,1)}, u32[]{:S(2)}, u32[]{:S(2)}) collective-permute-start(bf16[64,2048]{0,1:T(8,128)(2,1)} %collective-permute-done.10), channel_id=1, source_target_pairs={{0,1},{1,2},{2,3},{3,4},{4,5},{5,6},{6,7},{7,8},{8,9},{9,10},{10,1... | collective-permute-start | bytes 786440 | tf_op jit(solution)/shard_map/ppermute | solution.py:19
  236.4 17.1 %copy-start.6 = (bf16[64,2048]{0,1:T(8,128)(2,1)S(1)}, bf16[64,2048]{0,1:T(8,128)(2,1)}, u32[]{:S(2)}) copy-start(bf16[64,2048]{0,1:T(8,128)(2,1)} %copy-done.5) | copy-start | bytes 786436
  274.1 4.6 %copy-start.4 = (bf16[192,16,32]{2,0,1:T(8,128)(2,1)S(1)}, bf16[192,16,32]{2,0,1:T(8,128)(2,1)}, u32[]{:S(2)}) copy-start(bf16[192,16,32]{2,0,1:T(8,128)(2,1)} %get-tuple-element.20) | copy-start | bytes 589828
  278.8 3.2 slice-start
  278.8 3.3 slice-start.1
  282.0 4.6 %copy-start.2 = (f32[16,192,1024]{2,1,0:T(8,128)}, f32[16,192,1024]{2,1,0:T(8,128)S(1)}, u32[]{:S(2)}) copy-start(f32[16,192,1024]{2,1,0:T(8,128)S(1)} %get-tuple-element.31) | copy-start | bytes 37748740
  310.2 36.0 %copy-start.1 = (bf16[192,2048]{1,0:T(8,128)(2,1)S(1)}, bf16[192,2048]{1,0:T(8,128)(2,1)}, u32[]{:S(2)}) copy-start(bf16[192,2048]{1,0:T(8,128)(2,1)} %param.9) | copy-start | bytes 2359300
Sparse Core Ops, SparseCore 0:
  10.1 161.1 all-gather.1
  320.8 25.3 reduce-scatter.1
